TPU v7x, 32 devices: a whole 2x2x4 slice. The times are simulated.
32 devices in a mesh: groups: 2 (over y), seq: 16 (over z, x, core).
Axes of the slice: x: 2, y: 2, z: 4, core: 2. Of those that a mesh axis runs over, the one named last changes fastest.
Arguments:
- queries: bfloat16 [32, 16384], P(('groups', 'seq')), parts along dimension 0, may hold values from -8 to 8
- prompt_keys: bfloat16 [8192, 1024], P(('groups', 'seq')), parts along dimension 0, may hold values from -16 to 16
- prompt_values: bfloat16 [8192, 1024], P(('groups', 'seq')), parts along dimension 0, may hold values from -6 to 6
- suffix_keys: bfloat16 [32, 8, 64, 1024], P(('groups', 'seq')), parts along dimension 0, may hold values from -16 to 16
- suffix_values: bfloat16 [32, 8, 64, 1024], P(('groups', 'seq')), parts along dimension 0, may hold values from -6 to 6
- suffix_lengths: int32 [32], P(('groups', 'seq')), parts along dimension 0, may hold values from 1 to 512, 5120 in all
- block_tables: int32 [32, 8], P(('groups', 'seq')), parts along dimension 0, may hold values from 0 to 7, each once within a row
Outputs:
- attended: bfloat16 [32, 16384], P(('groups', 'seq')), parts along dimension 0
There are 2 independent parts, one for each index of `groups`. A program takes and returns all parts, laid end to end along the dimension named above; each array names one. Nothing has to cross between parts.
Inputs may be any that keep to these rules, and one draw needn't show every extreme that they name: `suffix_lengths`: in each group, one sample has exactly 512 live suffix positions, and the lengths of the group's 16 samples sum to 5120. `block_tables`: each row names every one of the sample's 8 pages once.
All inputs are finite; a program needn't handle non-finite values.
Results may differ from a plain program's by a relative error of at most 0.0025.
Values may be sent and summed in bfloat16 or wider, within the bound.
A program may use at most 64 MiB of HBM per device.

v0:
```python
import math

import jax
import jax.numpy as jnp
from jax import lax
from jax.sharding import PartitionSpec as P

H = 128
KVH = 8
HD = 128


def prompt_partial(query_block, key_rows, value_rows):
    scores = jnp.einsum(
        "skgd,pkd->skgp", query_block, key_rows, preferred_element_type=jnp.float32
    ) * (1.0 / math.sqrt(HD))
    maxima = jnp.max(scores, axis=-1)
    expos = jnp.exp(scores - maxima[..., None])
    totals = jnp.sum(expos, axis=-1)
    weights = expos.astype(jnp.bfloat16)
    numerators = jnp.einsum(
        "skgp,pkd->skgd", weights, value_rows, preferred_element_type=jnp.float32
    )
    return (maxima, totals, numerators)


def suffix_partial(query_heads, key_pages, value_pages, live_mask):
    scores = jnp.einsum(
        "skgd,stkd->skgt", query_heads, key_pages, preferred_element_type=jnp.float32
    ) * (1.0 / math.sqrt(HD))
    scores = jnp.where(live_mask[:, None, None, :], scores, -jnp.inf)
    maxima = jnp.max(scores, axis=-1)
    expos = jnp.exp(scores - maxima[..., None])
    totals = jnp.sum(expos, axis=-1)
    weights = expos.astype(jnp.bfloat16)
    numerators = jnp.einsum(
        "skgt,stkd->skgd", weights, value_pages, preferred_element_type=jnp.float32
    )
    return (maxima, totals, numerators)


def per_device(
    queries, prompt_keys, prompt_values, suffix_keys, suffix_values, suffix_lengths, block_tables
):
    own_count = queries.shape[0]
    per_kv = H // KVH
    everyone = lax.all_gather(queries, "seq", axis=0, tiled=True)
    samples = everyone.shape[0]
    key_rows = prompt_keys.reshape(-1, KVH, HD)
    value_rows = prompt_values.reshape(-1, KVH, HD)
    blocked = everyone.reshape(samples // 16, 16, KVH, per_kv, HD)
    maxima, totals, numerators = lax.map(
        lambda sample_block: prompt_partial(sample_block, key_rows, value_rows), blocked
    )
    maxima = maxima.reshape(samples, H)
    totals = totals.reshape(samples, H)
    numerators = numerators.reshape(samples, H * HD)
    got_max, got_total, got_num = (
        lax.all_to_all(maxima, "seq", split_axis=0, concat_axis=0, tiled=True),
        lax.all_to_all(totals, "seq", split_axis=0, concat_axis=0, tiled=True),
        lax.all_to_all(numerators, "seq", split_axis=0, concat_axis=0, tiled=True),
    )
    sources = lax.axis_size("seq")
    got_max = got_max.reshape(sources, own_count, H)
    prompt_max = jnp.max(got_max, axis=0)
    scaling = jnp.exp(got_max - prompt_max[None])
    prompt_total = jnp.sum(got_total.reshape(sources, own_count, H) * scaling, axis=0)
    prompt_num = jnp.sum(got_num.reshape(sources, own_count, H, HD) * scaling[..., None], axis=0)
    query_heads = queries.reshape(own_count, KVH, per_kv, HD)
    picker = block_tables[:, :, None, None]
    key_pages = jnp.take_along_axis(suffix_keys, picker, axis=1).reshape(own_count, -1, KVH, HD)
    value_pages = jnp.take_along_axis(suffix_values, picker, axis=1).reshape(own_count, -1, KVH, HD)
    positions = lax.broadcasted_iota(jnp.int32, (own_count, key_pages.shape[1]), 1)
    live_mask = positions < suffix_lengths[:, None]
    suffix_max, suffix_total, suffix_num = suffix_partial(
        query_heads, key_pages, value_pages, live_mask
    )
    suffix_max = suffix_max.reshape(own_count, H)
    suffix_total = suffix_total.reshape(own_count, H)
    suffix_num = suffix_num.reshape(own_count, H, HD)
    overall = jnp.maximum(prompt_max, suffix_max)
    prompt_scale = jnp.exp(prompt_max - overall)
    suffix_scale = jnp.exp(suffix_max - overall)
    numer_sum = prompt_num * prompt_scale[..., None] + suffix_num * suffix_scale[..., None]
    denom_sum = prompt_total * prompt_scale + suffix_total * suffix_scale
    attended = numer_sum / denom_sum[..., None]
    return attended.reshape(own_count, H * HD).astype(jnp.bfloat16)


def solution(mesh):
    placed = (
        P(("groups", "seq"), None),
        P(("groups", "seq"), None),
        P(("groups", "seq"), None),
        P(("groups", "seq"), None, None, None),
        P(("groups", "seq"), None, None, None),
        P(("groups", "seq")),
        P(("groups", "seq"), None),
    )
    return jax.shard_map(
        per_device,
        mesh=mesh,
        in_specs=placed,
        out_specs=P(("groups", "seq"), None),
        check_vma=False,
    )
```

profile of v0, /device:TPU:0, one launch (start us, length us, event | category | flops | bytes accessed | tf_op | source)
XLA Modules:
  0.0 85.4 jit_solution(12915089273070715917)
XLA Ops:
  0.0 0.0 copy-start
  0.0 2.0 %copy.46 = bf16[32,8,8,128]{3,2,1,0:T(8,128)(2,1)} copy(bf16[32,8,8,128]{3,1,2,0:T(8,128)(2,1)} %bitcast.83) | data formatting | bytes 1048576
  2.0 26.4 %all-gather = bf16[16,1,16384]{2,1,0:T(2,128)(2,1)S(1)} all-gather(bf16[1,1,16384]{2,1,0:T(2,128)(2,1)} %bitcast.85), channel_id=1, replica_groups=mesh['groups'=2,'seq'=16] {'seq'}, dimensions={0}, use_global_device_ids=true | all-gather | bytes 557056 | tf_op jit(solution)/shard_map/all_gather | solution.py:47
  28.4 3.1 %reduce.9 = bf16[16,16384]{1,0:T(8,128)(2,1)S(1)} reduce(bf16[16,1,16384]{2,1,0:T(2,128)(2,1)S(1)} %all-gather, bf16[]{:T(256)} %constant.41), dimensions={1}, to_apply=%all-gather.reduce_sub_computation | reduce | bytes 1048578 | tf_op jit(solution)/shard_map/all_gather | solution.py:47
  31.5 0.1 copy.47
  31.6 1.6 %bitcast_reduce_fusion = (f32[16,8,16]{2,0,1:T(8,128)S(1)}, f32[8,256,16,16]{1,3,2,0:T(8,128)S(1)}) fusion(bf16[16,8,16,128]{3,2,1,0:T(8,128)(2,1)S(1)} %bitcast.79, bf16[256,8,128,1]{2,1,0,3:T(8,128)(2,1)} %bitcast.78), kind=kOutput, calls=%fused_computation.3 | convolution fusion | flops 135264256 | bytes 3153920 | tf_op jit(solution)/shard_map/while/body/eval_jaxpr/skgd,pkd->skgp/dot_general | solution.py:14
  33.2 0.7 fusion.1
  34.0 0.7 all_to_all.25
  34.7 3.5 %all-to-all-start.2 = ((f32[16,1,128]{2,1,0:T(1,128)}), f32[16,1,128]{2,1,0:T(1,128)S(1)}, u32[]{:S(2)}, u32[]{:S(2)}) async-start(f32[16,1,128]{2,1,0:T(1,128)} %bitcast.23), calls=%async_computation.2 | async-start | bytes 16384 | tf_op jit(solution)/shard_map/all_to_all | solution.py:60
  38.2 1.9 %copy.48 = bf16[32,8,8,128]{3,2,1,0:T(8,128)(2,1)} copy(bf16[32,8,8,128]{3,1,2,0:T(8,128)(2,1)} %bitcast.84) | data formatting | bytes 1048576
  40.1 0.7 all_to_all.23
  40.8 3.7 %all-to-all-done.2 = f32[16,1,128]{2,1,0:T(1,128)S(1)} async-done(((f32[16,1,128]{2,1,0:T(1,128)}), f32[16,1,128]{2,1,0:T(1,128)S(1)}, u32[]{:S(2)}, u32[]{:S(2)}) %all-to-all-start.2) | async-done | bytes 8224 | tf_op jit(solution)/shard_map/all_to_all | solution.py:60
  44.5 3.5 %all-to-all-start.1 = ((f32[16,1,128]{2,1,0:T(1,128)}), f32[16,1,128]{2,1,0:T(1,128)S(1)}, u32[]{:S(2)}, u32[]{:S(2)}) async-start(f32[16,1,128]{2,1,0:T(1,128)} %bitcast.6), calls=%async_computation.1 | async-start | bytes 16384 | tf_op jit(solution)/shard_map/all_to_all | solution.py:59
  48.0 1.6 %convolution_bitcast_fusion = f32[16,8,16,128]{3,2,0,1:T(8,128)S(1)} fusion(f32[8,256,16,16]{1,3,2,0:T(8,128)S(1)} %get-tuple-element.37, f32[16,8,16]{2,0,1:T(8,128)S(1)} %get-tuple-element.36, bf16[256,8,128,1]{2,1,0,3:T(8,128)(2,1)} %bitcast.77), kind=kOutput, calls=%fused_computation.7 | convolution fusion | flops 135790592 | bytes 3678208 | tf_op jit(solution)/shard_map/while/body/eval_jaxpr/skgp,pkd->skgd/dot_general | solution.py:21
  49.6 0.0 copy-start.2
  49.6 0.0 copy-start.1
  49.6 1.1 %copy.31 = f32[16,8,16,128]{3,2,1,0:T(8,128)} copy(f32[16,8,16,128]{3,2,0,1:T(8,128)S(1)} %convolution_bitcast_fusion) | data formatting | bytes 2097152 | tf_op jit(solution)/shard_map/while/body/eval_jaxpr/skgp,pkd->skgd/transpose | solution.py:21
  50.7 3.7 %all-to-all-done.1 = f32[16,1,128]{2,1,0:T(1,128)S(1)} async-done(((f32[16,1,128]{2,1,0:T(1,128)}), f32[16,1,128]{2,1,0:T(1,128)S(1)}, u32[]{:S(2)}, u32[]{:S(2)}) %all-to-all-start.1) | async-done | bytes 8224 | tf_op jit(solution)/shard_map/all_to_all | solution.py:59
  54.4 4.3 %all-to-all-start = ((f32[16,1,16384]{2,1,0:T(1,128)}), f32[16,1,16384]{2,1,0:T(1,128)}, u32[]{:S(2)}, u32[]{:S(2)}) async-start(f32[16,1,16384]{2,1,0:T(1,128)} %bitcast.5), calls=%async_computation | async-start | bytes 2097152 | tf_op jit(solution)/shard_map/all_to_all | solution.py:61
  58.7 0.0 copy-done.2
  58.7 0.0 copy-done.1
  58.8 0.2 reduce.10
  59.6 0.0 copy-done
  59.6 0.6 gather_fusion.1
  60.2 1.8 %gather_fusion = bf16[8,64,1024]{2,1,0:T(8,128)(2,1)S(1)} fusion(bf16[8,64,1024]{2,1,0:T(8,128)(2,1)} %bitcast.81, s32[1024]{0:T(1024)S(1)} %pad_clamp_fusion), kind=kCustom, calls=%fused_computation.clone | custom fusion | bytes 2097184 | tf_op jit(solution)/shard_map/jit(take_along_axis)/gather | solution.py:71
  62.1 0.3 bitcast_select_fusion
  62.4 0.3 copy.51
  62.6 0.3 copy.50
  62.9 0.5 fusion.27
  63.4 0.1 reshape.291
  63.5 0.2 fusion.16
  63.7 0.1 reshape.294
  63.8 0.3 fusion.7
  64.2 17.4 %all-to-all-done = f32[16,1,16384]{2,1,0:T(1,128)} async-done(((f32[16,1,16384]{2,1,0:T(1,128)}), f32[16,1,16384]{2,1,0:T(1,128)}, u32[]{:S(2)}, u32[]{:S(2)}) %all-to-all-start) | async-done | bytes 1048608 | tf_op jit(solution)/shard_map/all_to_all | solution.py:61
  81.6 0.3 mul.96
  81.9 2.5 %fusion.6 = f32[16384]{0:T(1024)S(1)} fusion(f32[2,8,128,128]{3,2,1,0:T(8,128)S(1)} %bitcast.76, f32[16,1,16384]{2,1,0:T(1,128)} %all-to-all-done), kind=kLoop, calls=%fused_computation.12 | loop fusion | flops 507904 | bytes 2162688 | tf_op jit(solution)/shard_map/reduce_sum | solution.py:68
  84.4 0.1 div.20
  84.5 0.1 mul.101
  84.6 0.1 mul.104
  84.6 0.8 fusion.20
  (9 shorter events, 0.2 us)
Async XLA Ops:
  0.0 59.6 %copy-start = (bf16[1,8,64,1024]{3,2,1,0:T(8,128)(2,1)S(1)}, bf16[1,8,64,1024]{3,2,1,0:T(8,128)(2,1)}, u32[]{:S(2)}) copy-start(bf16[1,8,64,1024]{3,2,1,0:T(8,128)(2,1)} %param.13) | copy-start | bytes 3145732
  34.7 9.8 %all-to-all-start.2 = ((f32[16,1,128]{2,1,0:T(1,128)}), f32[16,1,128]{2,1,0:T(1,128)S(1)}, u32[]{:S(2)}, u32[]{:S(2)}) async-start(f32[16,1,128]{2,1,0:T(1,128)} %bitcast.23), calls=%async_computation.2 | async-start | bytes 16384 | tf_op jit(solution)/shard_map/all_to_all | solution.py:60
  44.5 9.9 %all-to-all-start.1 = ((f32[16,1,128]{2,1,0:T(1,128)}), f32[16,1,128]{2,1,0:T(1,128)S(1)}, u32[]{:S(2)}, u32[]{:S(2)}) async-start(f32[16,1,128]{2,1,0:T(1,128)} %bitcast.6), calls=%async_computation.1 | async-start | bytes 16384 | tf_op jit(solution)/shard_map/all_to_all | solution.py:59
  49.6 9.1 %copy-start.2 = (s32[1,8]{1,0:T(1,128)S(1)}, s32[1,8]{1,0:T(1,128)}, u32[]{:S(2)}) copy-start(s32[1,8]{1,0:T(1,128)} %param.15) | copy-start | bytes 100
  49.6 9.1 %copy-start.1 = (bf16[1,16384]{1,0:T(2,128)(2,1)S(1)}, bf16[1,16384]{1,0:T(2,128)(2,1)}, u32[]{:S(2)}) copy-start(bf16[1,16384]{1,0:T(2,128)(2,1)} %param.9) | copy-start | bytes 98308
  54.4 27.2 %all-to-all-start = ((f32[16,1,16384]{2,1,0:T(1,128)}), f32[16,1,16384]{2,1,0:T(1,128)}, u32[]{:S(2)}, u32[]{:S(2)}) async-start(f32[16,1,16384]{2,1,0:T(1,128)} %bitcast.5), calls=%async_computation | async-start | bytes 2097152 | tf_op jit(solution)/shard_map/all_to_all | solution.py:61
where the time goes:
time: 87.1 us; the launch traced here: 85.4 us
  blocking collectives  26.4 us (30%)
  waiting for transfers between devices  24.8 us (28%)
  starting transfers between devices  11.3 us (13%)
  local copies, waits for them, and re-layouts  10.3 us (12%)
  other arithmetic  7.9 us (9%)
  matrix products  3.99 us (5%)
    all_gather x1, blocking collectives, per_device(): everyone = lax.all_gather(queries, 'seq', axis=0, tiled=True)  26.4 us
    all_to_all x1, waiting for transfers between devices, per_device(): lax.all_to_all(numerators, 'seq', split_axis=0, concat_axis=0, tiled=True)  17.4 us
    unnamed x11, local copies, waits for them, and re-layouts  4.6 us
    all_to_all x1, starting transfers between devices, per_device(): lax.all_to_all(numerators, 'seq', split_axis=0, concat_axis=0, tiled=True)  4.34 us
    all_to_all x1, waiting for transfers between devices, per_device(): lax.all_to_all(totals, 'seq', split_axis=0, concat_axis=0, tiled=True)  3.68 us
    all_to_all x1, waiting for transfers between devices, per_device(): lax.all_to_all(maxima, 'seq', split_axis=0, concat_axis=0, tiled=True)  3.66 us
    all_to_all x1, starting transfers between devices, per_device(): lax.all_to_all(maxima, 'seq', split_axis=0, concat_axis=0, tiled=True)  3.49 us
    all_to_all x1, starting transfers between devices, per_device(): lax.all_to_all(totals, 'seq', split_axis=0, concat_axis=0, tiled=True)  3.47 us
  transfers between devices with their start and end apart: 3, of which 3 were waited for; matrix products, arithmetic and copies ran while one was open for 11% of the time, Pallas kernels for 0%

commit v1 on v0

v1 whole, which is shorter than its diff:
```python
import functools
import math

import jax
import jax.numpy as jnp
from jax import lax
from jax.experimental import pallas as pl
from jax.experimental.pallas import tpu as pltpu
from jax.sharding import PartitionSpec as P

H = 128
KVH = 8
HD = 128
G = H // KVH
HALF = H // 2
HK = KVH // 2
LINK = jnp.int16
FULL = 32767.0
LOG2 = math.log2(math.e) / math.sqrt(HD)
NT = (((1,), (1,)), ((), ()))


def kernel(
    n, lens, tables, q, k, v, sk, sv, out,
    qbuf, kbuf, vbuf, skb, svb, osend, orecv, ssend, srecv, osuf, lsuf,
    q_send, q_recv, o_send, o_recv, s_send, s_recv, kv_send, kv_recv, own_sem,
):
    me = lax.axis_index("seq")
    core = lax.rem(me, 2)
    partner = me + 1 - 2 * core
    rows = k.shape[0]
    width = k.shape[1] // 2
    nb = n // 4
    mine = me // 4

    def remote(src, dst, send, recv, peer):
        return pltpu.make_async_remote_copy(
            src_ref=src, dst_ref=dst, send_sem=send, recv_sem=recv,
            device_id={"seq": peer}, device_id_type=pl.DeviceIdType.MESH,
        )

    own_cols = pl.ds(pl.multiple_of(core * width, width), width)
    own_half = pl.ds(pl.multiple_of(core * HALF, HALF), HALF)
    local = [
        pltpu.make_async_copy(sk.at[0], skb, own_sem.at[0]),
        pltpu.make_async_copy(sv.at[0], svb, own_sem.at[1]),
        pltpu.make_async_copy(k.at[:, own_cols], kbuf.at[pl.ds(0, rows)], own_sem.at[2]),
        pltpu.make_async_copy(v.at[:, own_cols], vbuf.at[pl.ds(0, rows)], own_sem.at[3]),
        pltpu.make_async_copy(q.at[own_half], qbuf.at[me], own_sem.at[4]),
    ]
    for copy in local:
        copy.start()

    barrier = pltpu.get_barrier_semaphore()

    @pl.loop(1, n)
    def _(step):
        pl.semaphore_signal(
            barrier, inc=1, device_id={"seq": lax.rem(me + step, n)},
            device_id_type=pl.DeviceIdType.MESH,
        )

    pl.semaphore_wait(barrier, n - 1)

    def peer_of(i):
        group = lax.rem(mine + nb - i // 4, nb)
        return group * 4 + lax.rem(me + i, 4)

    def q_copy(peer):
        cut = pl.ds(pl.multiple_of(lax.rem(peer, 2) * HALF, HALF), HALF)
        return remote(q.at[cut], qbuf.at[me], q_send.at[peer], q_recv.at[me], peer)

    @pl.loop(1, n)
    def _(i):
        q_copy(peer_of(i)).start()

    away_cols = pl.ds(pl.multiple_of((1 - core) * width, width), width)
    kv = [
        remote(k.at[:, away_cols], kbuf.at[pl.ds(rows, rows)], kv_send.at[0], kv_recv.at[0], partner),
        remote(v.at[:, away_cols], vbuf.at[pl.ds(rows, rows)], kv_send.at[1], kv_recv.at[1], partner),
    ]
    for copy in kv:
        copy.start()

    pages, page = skb.shape[0], skb.shape[1]
    slots = pages * page
    lane = lax.broadcasted_iota(jnp.int32, (1, slots), 1)
    at_page = lane // page
    position = lane - at_page * page
    for j in range(pages):
        position = position + jnp.where(at_page == tables[0, j], j * page, 0)
    live = position < lens[0]
    for copy in local[:2]:
        copy.wait()
    for h in range(KVH):
        cols = pl.ds(h * HD, HD)
        keys = skb[:, :, cols].reshape(slots, HD)
        values = svb[:, :, cols].reshape(slots, HD)
        part = pl.ds(h * G, G)
        scores = lax.dot_general(q[part], keys, NT, preferred_element_type=jnp.float32)
        scores = jnp.where(live, scores, -jnp.inf)
        top = jnp.max(scores, axis=1, keepdims=True)
        expos = jnp.exp2((scores - top) * LOG2)
        total = jnp.sum(expos, axis=1, keepdims=True)
        num = jnp.dot(expos.astype(jnp.bfloat16), values, preferred_element_type=jnp.float32)
        osuf[part] = num / total
        lsuf[part] = jnp.broadcast_to(top * LOG2 + jnp.log2(total), (G, HD))

    for copy in local[2:]:
        copy.wait()
    for copy in kv:
        copy.wait_recv()

    def o_copy(peer):
        return remote(osend.at[peer], orecv.at[me], o_send.at[peer], o_recv.at[me], peer)

    def s_copy(peer):
        return remote(ssend.at[peer], srecv.at[me], s_send.at[peer], s_recv.at[me], peer)

    wide = lax.broadcasted_iota(jnp.int32, (G, HD), 1)

    def spread(column):
        tile = jnp.zeros((G, HD), jnp.float32)
        for s in range(4):
            tile = jnp.where(wide == s, column[s * G:(s + 1) * G], tile)
        return tile

    def batch(b, first):
        group = lax.rem(mine + b, nb)
        for j in range(1 if first else 0, 4):
            source = group * 4 + lax.rem(me + j, 4)
            remote(qbuf.at[source], qbuf.at[source], q_send.at[source], q_recv.at[source], partner).wait_recv()
        four = pl.ds(pl.multiple_of(group * 4, 4), 4)
        lses, steps = [], []
        for h in range(HK):
            cols = pl.ds(h * HD, HD)
            asked = qbuf[four, pl.ds(h * G, G), :].reshape(4 * G, HD)
            scores = lax.dot_general(asked, kbuf[:, cols], NT, preferred_element_type=jnp.float32)
            top = jnp.max(scores, axis=1, keepdims=True)
            expos = jnp.exp2((scores - top) * LOG2)
            total = jnp.sum(expos, axis=1, keepdims=True)
            num = jnp.dot(expos.astype(jnp.bfloat16), vbuf[:, cols], preferred_element_type=jnp.float32)
            peak = jnp.maximum(jnp.max(jnp.abs(num), axis=1, keepdims=True), 1e-30)
            fixed = jnp.round(num * (FULL / peak)).astype(jnp.int32).astype(LINK)
            osend[four, pl.ds(h * G, G), :] = fixed.reshape(4, G, HD)
            lses.append(spread(top * LOG2 + jnp.log2(total)))
            steps.append(spread(peak / (FULL * total)))
        flat = jnp.concatenate(lses + steps, axis=0).T
        for s in range(4):
            ssend[group * 4 + s] = flat[s:s + 1]
        for j in range(1 if first else 0, 4):
            peer = group * 4 + lax.rem(me + j, 4)
            o_copy(peer).start()
            s_copy(peer).start()
        if first:
            pltpu.make_async_copy(osend.at[me], orecv.at[me], own_sem.at[5]).start()
            pltpu.make_async_copy(ssend.at[me], srecv.at[me], own_sem.at[6]).start()

    batch(0, True)

    @pl.loop(1, nb)
    def _(b):
        batch(b, False)

    pltpu.make_async_copy(osend.at[me], orecv.at[me], own_sem.at[5]).wait()
    pltpu.make_async_copy(ssend.at[me], srecv.at[me], own_sem.at[6]).wait()

    @pl.loop(1, n)
    def _(i):
        source = lax.rem(me + i, n)
        s_copy(source).wait_send()
        remote(ssend.at[source], srecv.at[source], s_send.at[source], s_recv.at[source], partner).wait_recv()

    flat = srecv[...].reshape(n, HD)
    if n % HD:
        flat = jnp.concatenate([flat, jnp.zeros((HD - n % HD, HD), jnp.float32)], axis=0)
    turned = flat.T
    lse, steps = turned[:HALF], turned[HALF:]
    from_lane = lax.broadcasted_iota(jnp.int32, lse.shape, 1)

    @pl.loop(1, n)
    def _(i):
        source = lax.rem(me + i, n)
        o_copy(source).wait_send()
        remote(osend.at[source], orecv.at[source], o_send.at[source], o_recv.at[source], partner).wait_recv()

    for half in range(2):
        part = pl.ds(half * HALF, HALF)
        ok = jnp.logical_and(lax.rem(from_lane, 2) == half, from_lane < n)
        there = jnp.where(ok, lse, -jnp.inf)
        suffix = lsuf[part]
        top = jnp.maximum(jnp.max(there, axis=1, keepdims=True), suffix[:, :1])
        weight = jnp.exp2(there - top)
        own = jnp.exp2(suffix[:, :1] - top)
        total = jnp.sum(weight, axis=1, keepdims=True) + own
        weight = weight * jnp.where(ok, steps, 0.0)
        acc = osuf[part] * own
        for chip in range(n // 2):
            source = 2 * chip + half
            acc = acc + weight[:, source:source + 1] * orecv[source].astype(jnp.float32)
        out[part] = (acc / total).astype(jnp.bfloat16)

    for copy in kv:
        copy.wait_send()

    @pl.loop(1, n)
    def _(i):
        q_copy(peer_of(i)).wait_send()


def per_device(n, queries, keys, values, suffix_keys, suffix_values, lengths, tables):
    rows = keys.shape[0]
    pages, page, width = suffix_keys.shape[1:]
    dma = pltpu.SemaphoreType.DMA
    anywhere = pl.BlockSpec(memory_space=pl.ANY)
    scalar = pl.BlockSpec(memory_space=pltpu.SMEM)
    vector = pl.BlockSpec(memory_space=pltpu.VMEM)
    out = pl.pallas_call(
        functools.partial(kernel, n),
        out_shape=jax.ShapeDtypeStruct((H, HD), jnp.bfloat16),
        in_specs=[scalar, scalar, vector, anywhere, anywhere, anywhere, anywhere],
        out_specs=vector,
        scratch_shapes=[
            pltpu.VMEM((n, HALF, HD), jnp.bfloat16),
            pltpu.VMEM((2 * rows, width // 2), jnp.bfloat16),
            pltpu.VMEM((2 * rows, width // 2), jnp.bfloat16),
            pltpu.VMEM((pages, page, width), jnp.bfloat16),
            pltpu.VMEM((pages, page, width), jnp.bfloat16),
            pltpu.VMEM((n, HALF, HD), LINK),
            pltpu.VMEM((n, HALF, HD), LINK),
            pltpu.VMEM((n, 1, HD), jnp.float32),
            pltpu.VMEM((n, 1, HD), jnp.float32),
            pltpu.VMEM((H, HD), jnp.float32),
            pltpu.VMEM((H, HD), jnp.float32),
            dma((n,)), dma((n,)), dma((n,)), dma((n,)), dma((n,)), dma((n,)),
            dma((2,)), dma((2,)), dma((7,)),
        ],
        compiler_params=pltpu.CompilerParams(collective_id=0, has_side_effects=True),
        name="attend",
    )(lengths, tables, queries.reshape(H, HD), keys, values, suffix_keys, suffix_values)
    return out.reshape(1, H * HD)


def solution(mesh):
    rows = P(("groups", "seq"), None)
    pages = P(("groups", "seq"), None, None, None)
    return jax.shard_map(
        functools.partial(per_device, mesh.shape["seq"]),
        mesh=mesh,
        in_specs=(rows, rows, rows, pages, pages, P(("groups", "seq")), rows),
        out_specs=rows,
        check_vma=False,
    )
```

time: 87.1 us -> 28.8 us (0.33); the launches traced: 85.4 us -> 28.5 us
  blocking collectives: 26.4 us -> 0 us
  Pallas kernels: 0 us -> 24.8 us
  waiting for transfers between devices: 24.8 us -> 0 us
  starting transfers between devices: 11.3 us -> 0 us
  local copies, waits for them, and re-layouts: 10.3 us -> 1.44 us
  other arithmetic: 7.9 us -> 1.63 us
  matrix products: 3.99 us -> 0 us
    all_gather x1 -> x0, blocking collectives: 26.4 us -> none  [per_device(): everyone = lax.all_gather(queries, 'seq', axis=0, tiled=True)]
    pallas_call x0 -> x1, Pallas kernels: none -> 24.8 us  [per_device(): pl.pallas_call(functools.partial(kernel, n), out_shape=jax.ShapeDtypeStru...]
    all_to_all x3 -> x0, waiting for transfers between devices: 24.8 us -> none  [the longest x1 17.4 us: per_device(): lax.all_to_all(numerators, 'seq', split_axis=0, concat_axis=0, tiled=True)]
    all_to_all x3 -> x0, starting transfers between devices: 11.3 us -> none  [the longest x1 4.34 us: per_device(): lax.all_to_all(numerators, 'seq', split_axis=0, concat_axis=0, tiled=True)]
    dot_general x4 -> x0, matrix products: 3.99 us -> none  [the longest x1 1.62 us: prompt_partial(): jnp.einsum('skgp,pkd->skgd', weights, value_rows, preferred_element_type=...]
    reduce_sum x4 -> x0, other arithmetic: 3.45 us -> none  [the longest x1 2.45 us: per_device(): jnp.sum(got_num.reshape(sources, own_count, H, HD) * scaling[..., None],...]
    unnamed x11 -> x1, local copies, waits for them, and re-layouts: 4.6 us -> 1.44 us
    all_gather x1 -> x0, other arithmetic: 3.14 us -> none  [per_device(): everyone = lax.all_gather(queries, 'seq', axis=0, tiled=True)]
  transfers between devices with their start and end apart: 3 -> 0, of which waited for: 3 -> 0; matrix products, arithmetic and copies ran while one was open for 11% -> 0% of each run, Pallas kernels for 0% -> 0%
where the time goes in v1:
time: 28.8 us; the launch traced here: 28.5 us
  Pallas kernels  24.8 us (86%)
  other arithmetic  1.63 us (6%)
  local copies, waits for them, and re-layouts  1.44 us (5%)
  between operations  0.66 us (2%)
    pallas_call x1, Pallas kernels, per_device(): pl.pallas_call(functools.partial(kernel, n), out_shape=jax.ShapeDtypeStru...  24.8 us
    unnamed x1, other arithmetic  1.63 us
    unnamed x1, local copies, waits for them, and re-layouts  1.44 us

profile of v1, /device:TPU:0, one launch (start us, length us, event | category | flops | bytes accessed | tf_op | source)
XLA Modules:
  0.0 28.5 jit_solution(16751941973211789455)
XLA Ops:
  0.7 1.6 %reduce = bf16[16384]{0:T(1024)(128)(2,1)} reduce(bf16[1,16384]{1,0:T(2,128)(2,1)} %param.7, bf16[]{:T(256)} %constant.5), dimensions={0}, to_apply=%param.7.reduce_sub_computation | reduce | bytes 65538 | tf_op args[0]
  2.3 24.8 %attend.1 = bf16[128,128]{1,0:T(8,128)(2,1)} custom-call(s32[1]{0:T(128)S(6)} %copy.11.lens, s32[1,8]{1,0:T(1,128)} %tables.1, bf16[128,128]{1,0:T(8,128)(2,1)} %bitcast.6, bf16[256,1024]{1,0:T(8,128)(2,1)} %k.1, bf16[256,1024]{1,0:T(8,128)(2,1)} %v.1, bf16[1,8,64,1024]{3,2,1,0:T(8,128)(2,1)} %sk.1, bf16[1,8,64,1024]{3,2,1,0:T(8,128)(2,1)} %sv.1), custom_call_target="tpu_custom_call" | custom-call | tf_op jit(solution)/shard_map/attend/pallas_call | solution.py:218
  27.1 1.4 %copy.10 = bf16[1,1,128,128]{3,1,2,0:T(2,128)(2,1)} copy(bf16[1,1,128,128]{3,2,1,0:T(8,128)(2,1)} %bitcast.7) | data formatting | bytes 65536

commit v2 on v1

--- a/solution.py
+++ b/solution.py
@@ -15,14 +15,15 @@
 HALF = H // 2
 HK = KVH // 2
 LINK = jnp.int16
+UNROLL = 16
 FULL = 32767.0
 LOG2 = math.log2(math.e) / math.sqrt(HD)
 NT = (((1,), (1,)), ((), ()))
 
 
 def kernel(
-    n, lens, tables, q, k, v, sk, sv, out,
-    qbuf, kbuf, vbuf, skb, svb, osend, orecv, ssend, srecv, osuf, lsuf,
+    n, lens, tables, flat_q, k, v, sk, sv, out,
+    q, rows32, qbuf, kbuf, vbuf, skb, svb, osend, orecv, ssend, srecv, osuf, lsuf,
     q_send, q_recv, o_send, o_recv, s_send, s_recv, kv_send, kv_recv, own_sem,
 ):
     me = lax.axis_index("seq")
@@ -46,33 +47,41 @@
         pltpu.make_async_copy(sv.at[0], svb, own_sem.at[1]),
         pltpu.make_async_copy(k.at[:, own_cols], kbuf.at[pl.ds(0, rows)], own_sem.at[2]),
         pltpu.make_async_copy(v.at[:, own_cols], vbuf.at[pl.ds(0, rows)], own_sem.at[3]),
-        pltpu.make_async_copy(q.at[own_half], qbuf.at[me], own_sem.at[4]),
     ]
     for copy in local:
         copy.start()
 
     barrier = pltpu.get_barrier_semaphore()
 
-    @pl.loop(1, n)
-    def _(step):
-        pl.semaphore_signal(
-            barrier, inc=1, device_id={"seq": lax.rem(me + step, n)},
-            device_id_type=pl.DeviceIdType.MESH,
-        )
-
-    pl.semaphore_wait(barrier, n - 1)
+    def each(low, high, step):
+        if n <= UNROLL:
+            for i in range(low, high):
+                step(i)
+        else:
+            pl.loop(low, high)(step)
 
     def peer_of(i):
         group = lax.rem(mine + nb - i // 4, nb)
         return group * 4 + lax.rem(me + i, 4)
 
+    def greet(i):
+        pl.semaphore_signal(
+            barrier, inc=1, device_id={"seq": peer_of(n - i)},
+            device_id_type=pl.DeviceIdType.MESH,
+        )
+
+    each(1, n, greet)
+    for h in range(H):
+        rows32[h:h + 1] = flat_q[:, h * HD:(h + 1) * HD].astype(jnp.float32)
+    q[...] = rows32[...].astype(jnp.bfloat16)
+    qbuf[me] = q[own_half]
+    pl.semaphore_wait(barrier, n - 1)
+
     def q_copy(peer):
         cut = pl.ds(pl.multiple_of(lax.rem(peer, 2) * HALF, HALF), HALF)
         return remote(q.at[cut], qbuf.at[me], q_send.at[peer], q_recv.at[me], peer)
 
-    @pl.loop(1, n)
-    def _(i):
-        q_copy(peer_of(i)).start()
+    each(1, n, lambda i: q_copy(peer_of(i)).start())
 
     away_cols = pl.ds(pl.multiple_of((1 - core) * width, width), width)
     kv = [
@@ -132,14 +141,16 @@
             remote(qbuf.at[source], qbuf.at[source], q_send.at[source], q_recv.at[source], partner).wait_recv()
         four = pl.ds(pl.multiple_of(group * 4, 4), 4)
         lses, steps = [], []
+        ones = jnp.ones((kbuf.shape[0], HD), jnp.bfloat16)
         for h in range(HK):
             cols = pl.ds(h * HD, HD)
             asked = qbuf[four, pl.ds(h * G, G), :].reshape(4 * G, HD)
             scores = lax.dot_general(asked, kbuf[:, cols], NT, preferred_element_type=jnp.float32)
             top = jnp.max(scores, axis=1, keepdims=True)
             expos = jnp.exp2((scores - top) * LOG2)
-            total = jnp.sum(expos, axis=1, keepdims=True)
-            num = jnp.dot(expos.astype(jnp.bfloat16), vbuf[:, cols], preferred_element_type=jnp.float32)
+            wider = jnp.concatenate([vbuf[:, cols], ones], axis=1)
+            both = jnp.dot(expos.astype(jnp.bfloat16), wider, preferred_element_type=jnp.float32)
+            num, total = both[:, :HD], both[:, HD:]
             peak = jnp.maximum(jnp.max(jnp.abs(num), axis=1, keepdims=True), 1e-30)
             fixed = jnp.round(num * (FULL / peak)).astype(jnp.int32).astype(LINK)
             osend[four, pl.ds(h * G, G), :] = fixed.reshape(4, G, HD)
@@ -158,54 +169,55 @@
 
     batch(0, True)
 
-    @pl.loop(1, nb)
-    def _(b):
-        batch(b, False)
-
-    pltpu.make_async_copy(osend.at[me], orecv.at[me], own_sem.at[5]).wait()
+    each(1, nb, lambda b: batch(b, False))
+
+    order = [lax.rem(mine + i // 4, nb) * 4 + lax.rem(me + i, 4) for i in range(n)]
     pltpu.make_async_copy(ssend.at[me], srecv.at[me], own_sem.at[6]).wait()
-
-    @pl.loop(1, n)
-    def _(i):
-        source = lax.rem(me + i, n)
-        s_copy(source).wait_send()
+    for source in order[1:]:
         remote(ssend.at[source], srecv.at[source], s_send.at[source], s_recv.at[source], partner).wait_recv()
-
-    flat = srecv[...].reshape(n, HD)
+    flat = [srecv[source] for source in order]
     if n % HD:
-        flat = jnp.concatenate([flat, jnp.zeros((HD - n % HD, HD), jnp.float32)], axis=0)
-    turned = flat.T
+        flat.append(jnp.zeros((HD - n % HD, HD), jnp.float32))
+    turned = jnp.concatenate(flat, axis=0).T
     lse, steps = turned[:HALF], turned[HALF:]
     from_lane = lax.broadcasted_iota(jnp.int32, lse.shape, 1)
-
-    @pl.loop(1, n)
-    def _(i):
-        source = lax.rem(me + i, n)
-        o_copy(source).wait_send()
-        remote(osend.at[source], orecv.at[source], o_send.at[source], o_recv.at[source], partner).wait_recv()
-
-    for half in range(2):
-        part = pl.ds(half * HALF, HALF)
-        ok = jnp.logical_and(lax.rem(from_lane, 2) == half, from_lane < n)
+    accs, weights, totals, parts = [], [], [], []
+    for side in range(2):
+        half = lax.rem(core + side, 2)
+        part = pl.ds(pl.multiple_of(half * HALF, HALF), HALF)
+        ok = jnp.logical_and(lax.rem(from_lane, 2) == side, from_lane < n)
         there = jnp.where(ok, lse, -jnp.inf)
         suffix = lsuf[part]
         top = jnp.maximum(jnp.max(there, axis=1, keepdims=True), suffix[:, :1])
         weight = jnp.exp2(there - top)
         own = jnp.exp2(suffix[:, :1] - top)
         total = jnp.sum(weight, axis=1, keepdims=True) + own
-        weight = weight * jnp.where(ok, steps, 0.0)
-        acc = osuf[part] * own
-        for chip in range(n // 2):
-            source = 2 * chip + half
-            acc = acc + weight[:, source:source + 1] * orecv[source].astype(jnp.float32)
-        out[part] = (acc / total).astype(jnp.bfloat16)
+        inverse = 1.0 / total
+        weights.append(weight * jnp.where(ok, steps, 0.0) * inverse)
+        accs.append(osuf[part] * (own * inverse))
+    pltpu.make_async_copy(osend.at[me], orecv.at[me], own_sem.at[5]).wait()
+    for i, source in enumerate(order):
+        if i:
+            remote(osend.at[source], orecv.at[source], o_send.at[source], o_recv.at[source], partner).wait_recv()
+        side = i % 2
+        accs[side] = accs[side] + weights[side][:, i:i + 1] * orecv[source].astype(jnp.float32)
+    for side in range(2):
+        base = lax.rem(core + side, 2) * HALF
+        done = accs[side]
+        for h in range(HALF):
+            at = pl.ds(pl.multiple_of((base + h) * HD, HD), HD)
+            out[:, at] = done[h:h + 1].astype(jnp.bfloat16)
 
     for copy in kv:
         copy.wait_send()
 
-    @pl.loop(1, n)
-    def _(i):
-        q_copy(peer_of(i)).wait_send()
+    def left(i):
+        peer = peer_of(i)
+        q_copy(peer).wait_send()
+        o_copy(peer).wait_send()
+        s_copy(peer).wait_send()
+
+    each(1, n, left)
 
 
 def per_device(n, queries, keys, values, suffix_keys, suffix_values, lengths, tables):
@@ -217,10 +229,12 @@
     vector = pl.BlockSpec(memory_space=pltpu.VMEM)
     out = pl.pallas_call(
         functools.partial(kernel, n),
-        out_shape=jax.ShapeDtypeStruct((H, HD), jnp.bfloat16),
+        out_shape=jax.ShapeDtypeStruct((1, H * HD), jnp.bfloat16),
         in_specs=[scalar, scalar, vector, anywhere, anywhere, anywhere, anywhere],
         out_specs=vector,
         scratch_shapes=[
+            pltpu.VMEM((H, HD), jnp.bfloat16),
+            pltpu.VMEM((H, HD), jnp.float32),
             pltpu.VMEM((n, HALF, HD), jnp.bfloat16),
             pltpu.VMEM((2 * rows, width // 2), jnp.bfloat16),
             pltpu.VMEM((2 * rows, width // 2), jnp.bfloat16),
@@ -237,8 +251,8 @@
         ],
         compiler_params=pltpu.CompilerParams(collective_id=0, has_side_effects=True),
         name="attend",
-    )(lengths, tables, queries.reshape(H, HD), keys, values, suffix_keys, suffix_values)
-    return out.reshape(1, H * HD)
+    )(lengths, tables, queries, keys, values, suffix_keys, suffix_values)
+    return out
 
 
 def solution(mesh):

time: 28.8 us -> 26.3 us (0.913)
  other arithmetic: 1.63 us -> 0 us
  Pallas kernels: 24.8 us -> 23.9 us
    unnamed x1 -> x0, other arithmetic: 1.63 us -> none
    pallas_call x1, Pallas kernels: 24.8 us -> 23.9 us  [per_device(): pl.pallas_call(functools.partial(kernel, n), out_shape=jax.ShapeDtypeStru...]
where the time goes in v2:
time: 26.3 us; the launch traced here: 26.1 us
  Pallas kernels  23.9 us (91%)
  local copies, waits for them, and re-layouts  1.54 us (6%)
  between operations  0.66 us (3%)
    pallas_call x1, Pallas kernels, per_device(): pl.pallas_call(functools.partial(kernel, n), out_shape=jax.ShapeDtypeStru...  23.9 us
    unnamed x1, local copies, waits for them, and re-layouts  1.54 us

profile of v2, /device:TPU:0, one launch (start us, length us, event | category | flops | bytes accessed | tf_op | source)
XLA Modules:
  0.0 26.1 jit_solution(11949781610267701785)
XLA Ops:
  0.7 23.9 %attend.1 = bf16[1,16384]{1,0:T(2,128)(2,1)} custom-call(s32[1]{0:T(128)S(6)} %copy.9.lens, s32[1,8]{1,0:T(1,128)} %tables.1, bf16[1,16384]{1,0:T(2,128)(2,1)} %flat_q.1, bf16[256,1024]{1,0:T(8,128)(2,1)} %k.1, bf16[256,1024]{1,0:T(8,128)(2,1)} %v.1, bf16[1,8,64,1024]{3,2,1,0:T(8,128)(2,1)} %sk.1, bf16[1,8,64,1024]{3,2,1,0:T(8,128)(2,1)} %sv.1), custom_call_target="tpu_custom_call" | custom-call | tf_op jit(solution)/shard_map/attend/pallas_call | solution.py:230
  24.5 1.5 %copy.10 = bf16[1,16384]{1,0:T(2,128)(2,1)} copy(bf16[1,16384]{1,0:T(2,128)(2,1)} %attend.1) | data formatting | bytes 65536

commit v3 on v2

--- a/solution.py
+++ b/solution.py
@@ -17,7 +17,7 @@
 LINK = jnp.int16
 UNROLL = 16
 FULL = 32767.0
-LOG2 = math.log2(math.e) / math.sqrt(HD)
+SCALE = 1.0 / math.sqrt(HD)
 NT = (((1,), (1,)), ((), ()))
 
 
@@ -75,22 +75,6 @@
         rows32[h:h + 1] = flat_q[:, h * HD:(h + 1) * HD].astype(jnp.float32)
     q[...] = rows32[...].astype(jnp.bfloat16)
     qbuf[me] = q[own_half]
-    pl.semaphore_wait(barrier, n - 1)
-
-    def q_copy(peer):
-        cut = pl.ds(pl.multiple_of(lax.rem(peer, 2) * HALF, HALF), HALF)
-        return remote(q.at[cut], qbuf.at[me], q_send.at[peer], q_recv.at[me], peer)
-
-    each(1, n, lambda i: q_copy(peer_of(i)).start())
-
-    away_cols = pl.ds(pl.multiple_of((1 - core) * width, width), width)
-    kv = [
-        remote(k.at[:, away_cols], kbuf.at[pl.ds(rows, rows)], kv_send.at[0], kv_recv.at[0], partner),
-        remote(v.at[:, away_cols], vbuf.at[pl.ds(rows, rows)], kv_send.at[1], kv_recv.at[1], partner),
-    ]
-    for copy in kv:
-        copy.start()
-
     pages, page = skb.shape[0], skb.shape[1]
     slots = pages * page
     lane = lax.broadcasted_iota(jnp.int32, (1, slots), 1)
@@ -109,11 +93,28 @@
         scores = lax.dot_general(q[part], keys, NT, preferred_element_type=jnp.float32)
         scores = jnp.where(live, scores, -jnp.inf)
         top = jnp.max(scores, axis=1, keepdims=True)
-        expos = jnp.exp2((scores - top) * LOG2)
+        expos = jnp.exp((scores - top) * SCALE)
         total = jnp.sum(expos, axis=1, keepdims=True)
         num = jnp.dot(expos.astype(jnp.bfloat16), values, preferred_element_type=jnp.float32)
         osuf[part] = num / total
-        lsuf[part] = jnp.broadcast_to(top * LOG2 + jnp.log2(total), (G, HD))
+        lsuf[part] = jnp.broadcast_to(top * SCALE + jnp.log(total), (G, HD))
+
+    pl.semaphore_wait(barrier, n - 1)
+
+    def q_copy(peer):
+        cut = pl.ds(pl.multiple_of(lax.rem(peer, 2) * HALF, HALF), HALF)
+        return remote(q.at[cut], qbuf.at[me], q_send.at[peer], q_recv.at[me], peer)
+
+    each(4, n, lambda i: q_copy(peer_of(i)).start())
+    each(1, 4, lambda i: q_copy(peer_of(i)).start())
+
+    away_cols = pl.ds(pl.multiple_of((1 - core) * width, width), width)
+    kv = [
+        remote(k.at[:, away_cols], kbuf.at[pl.ds(rows, rows)], kv_send.at[0], kv_recv.at[0], partner),
+        remote(v.at[:, away_cols], vbuf.at[pl.ds(rows, rows)], kv_send.at[1], kv_recv.at[1], partner),
+    ]
+    for copy in kv:
+        copy.start()
 
     for copy in local[2:]:
         copy.wait()
@@ -147,22 +148,22 @@
             asked = qbuf[four, pl.ds(h * G, G), :].reshape(4 * G, HD)
             scores = lax.dot_general(asked, kbuf[:, cols], NT, preferred_element_type=jnp.float32)
             top = jnp.max(scores, axis=1, keepdims=True)
-            expos = jnp.exp2((scores - top) * LOG2)
+            expos = jnp.exp((scores - top) * SCALE)
             wider = jnp.concatenate([vbuf[:, cols], ones], axis=1)
             both = jnp.dot(expos.astype(jnp.bfloat16), wider, preferred_element_type=jnp.float32)
             num, total = both[:, :HD], both[:, HD:]
             peak = jnp.maximum(jnp.max(jnp.abs(num), axis=1, keepdims=True), 1e-30)
             fixed = jnp.round(num * (FULL / peak)).astype(jnp.int32).astype(LINK)
             osend[four, pl.ds(h * G, G), :] = fixed.reshape(4, G, HD)
-            lses.append(spread(top * LOG2 + jnp.log2(total)))
+            lses.append(spread(top * SCALE + jnp.log(total)))
             steps.append(spread(peak / (FULL * total)))
         flat = jnp.concatenate(lses + steps, axis=0).T
         for s in range(4):
             ssend[group * 4 + s] = flat[s:s + 1]
         for j in range(1 if first else 0, 4):
             peer = group * 4 + lax.rem(me + j, 4)
+            s_copy(peer).start()
             o_copy(peer).start()
-            s_copy(peer).start()
         if first:
             pltpu.make_async_copy(osend.at[me], orecv.at[me], own_sem.at[5]).start()
             pltpu.make_async_copy(ssend.at[me], srecv.at[me], own_sem.at[6]).start()
@@ -189,8 +190,8 @@
         there = jnp.where(ok, lse, -jnp.inf)
         suffix = lsuf[part]
         top = jnp.maximum(jnp.max(there, axis=1, keepdims=True), suffix[:, :1])
-        weight = jnp.exp2(there - top)
-        own = jnp.exp2(suffix[:, :1] - top)
+        weight = jnp.exp(there - top)
+        own = jnp.exp(suffix[:, :1] - top)
         total = jnp.sum(weight, axis=1, keepdims=True) + own
         inverse = 1.0 / total
         weights.append(weight * jnp.where(ok, steps, 0.0) * inverse)
@@ -203,10 +204,7 @@
         accs[side] = accs[side] + weights[side][:, i:i + 1] * orecv[source].astype(jnp.float32)
     for side in range(2):
         base = lax.rem(core + side, 2) * HALF
-        done = accs[side]
-        for h in range(HALF):
-            at = pl.ds(pl.multiple_of((base + h) * HD, HD), HD)
-            out[:, at] = done[h:h + 1].astype(jnp.bfloat16)
+        out[pl.ds(pl.multiple_of(base, HALF), HALF)] = accs[side].astype(jnp.bfloat16)
 
     for copy in kv:
         copy.wait_send()
@@ -229,7 +227,7 @@
     vector = pl.BlockSpec(memory_space=pltpu.VMEM)
     out = pl.pallas_call(
         functools.partial(kernel, n),
-        out_shape=jax.ShapeDtypeStruct((1, H * HD), jnp.bfloat16),
+        out_shape=jax.ShapeDtypeStruct((H, HD), jnp.bfloat16),
         in_specs=[scalar, scalar, vector, anywhere, anywhere, anywhere, anywhere],
         out_specs=vector,
         scratch_shapes=[
@@ -252,7 +250,7 @@
         compiler_params=pltpu.CompilerParams(collective_id=0, has_side_effects=True),
         name="attend",
     )(lengths, tables, queries, keys, values, suffix_keys, suffix_values)
-    return out
+    return out.reshape(1, H * HD)
 
 
 def solution(mesh):

time: 26.3 us -> 25.5 us (0.970)
  Pallas kernels: 23.9 us -> 23 us
    pallas_call x1, Pallas kernels: 23.9 us -> 23 us  [per_device(): pl.pallas_call(functools.partial(kernel, n), out_shape=jax.ShapeDtypeStru...]
where the time goes in v3:
time: 25.5 us; the launch traced here: 25.1 us
  Pallas kernels  23 us (90%)
  local copies, waits for them, and re-layouts  1.44 us (6%)
  between operations  0.66 us (3%)
    pallas_call x1, Pallas kernels, per_device(): pl.pallas_call(functools.partial(kernel, n), out_shape=jax.ShapeDtypeStru...  23 us
    unnamed x1, local copies, waits for them, and re-layouts  1.44 us

profile of v3, /device:TPU:0, one launch (start us, length us, event | category | flops | bytes accessed | tf_op | source)
XLA Modules:
  0.0 25.1 jit_solution(12191943615712456483)
XLA Ops:
  0.7 23.0 %attend.1 = bf16[128,128]{1,0:T(8,128)(2,1)} custom-call(s32[1]{0:T(128)S(6)} %copy.11.lens, s32[1,8]{1,0:T(1,128)} %tables.1, bf16[1,16384]{1,0:T(2,128)(2,1)} %flat_q.1, bf16[256,1024]{1,0:T(8,128)(2,1)} %k.1, bf16[256,1024]{1,0:T(8,128)(2,1)} %v.1, bf16[1,8,64,1024]{3,2,1,0:T(8,128)(2,1)} %sk.1, bf16[1,8,64,1024]{3,2,1,0:T(8,128)(2,1)} %sv.1), custom_call_target="tpu_custom_call" | custom-call | tf_op jit(solution)/shard_map/attend/pallas_call | solution.py:228
  23.6 1.4 %copy.10 = bf16[1,1,128,128]{3,1,2,0:T(2,128)(2,1)} copy(bf16[1,1,128,128]{3,2,1,0:T(8,128)(2,1)} %bitcast.5) | data formatting | bytes 65536
